TPU v7x, 32 devices: a whole 2x2x4 slice. The times are simulated.
32 devices in a mesh: dp: 8 (over z, x), seq: 4 (over y, core).
Axes of the slice: x: 2, y: 2, z: 4, core: 2. Of those that a mesh axis runs over, the one named last changes fastest.
Arguments:
- inputs: bfloat16 [32, 1024, 1024], P('dp', 'seq'), may hold values from -6 to 6
- norm_gain: float32 [1024], replicated, may hold values from 0.1 to 1.9
- norm_shift: float32 [1024], replicated, may hold values from -3 to 3
- qkv_weight: bfloat16 [1024, 3072], replicated, may hold values from -0.1875 to 0.1875
- out_weight: bfloat16 [1024, 1024], replicated, may hold values from -0.75 to 0.75
- up_weight: bfloat16 [1024, 4096], replicated, may hold values from -0.1875 to 0.1875
- up_bias: float32 [4096], replicated, may hold values from -3 to 3
- down_weight: bfloat16 [4096, 1024], replicated, may hold values from -0.09375 to 0.09375
- down_bias: float32 [1024], replicated, may hold values from -3 to 3
- partners: int32 [32], P('dp'), may hold values from 0 to 31, as said below
- families: int32 [32, 1024], P('dp'), may hold values from 0 to 1023, as said below
- cotangent: bfloat16 [32, 1024, 1024], P('dp', 'seq'), may hold values from -6 to 6
Outputs:
- layer_out: bfloat16 [32, 1024, 1024], P('dp', 'seq')
- input_grad: float32 [32, 1024, 1024], P('dp', 'seq')
- gain_grad: float32 [1024], replicated
- shift_grad: float32 [1024], replicated
- qkv_grad: float32 [1024, 3072], P('dp', 'seq')
- out_grad: float32 [1024, 1024], P('dp', 'seq')
- up_grad: float32 [1024, 4096], P('dp', 'seq')
- up_bias_grad: float32 [4096], replicated
- down_grad: float32 [4096, 1024], P('dp', 'seq')
- down_bias_grad: float32 [1024], replicated
Inputs may be any that keep to these rules, and one draw needn't show every extreme that they name: partners pairs the rows of each aligned block of 4 rows two by two: partners[partners[r]] = r, partners[r] != r, and partners[r] lies in the block of r. `families`: family ids never fall along a row and the last position of every row has id 1024 - 1; in each aligned block of 4 rows at least one row is a single group over all 1024 positions.
All inputs are finite; a program needn't handle non-finite values.
Results may differ from a plain program's by a relative error of at most 0.0099.
Values may be sent and summed in bfloat16 or wider, within the bound.
A program may use at most 256 MiB of HBM per device.

v0:
```python
import jax
import jax.numpy as jnp
from jax import lax
from jax.sharding import PartitionSpec as P

HEADS = 16
HEAD_DIM = 64
ROT = 32


EPS = 1e-05


def norm_piece(values, norm_gain, norm_shift):
    row_mean = jnp.mean(values, -1, keepdims=True)
    centered = values - row_mean
    variance = jnp.mean(centered * centered, -1, keepdims=True)
    return centered * lax.rsqrt(variance + EPS) * norm_gain + norm_shift


def rotate(values, places):
    half_rot = ROT // 2
    inverse_freq = 10000.0 ** (-2.0 * jnp.arange(half_rot).astype(jnp.float32) / ROT)
    angles = places.astype(jnp.float32)[:, None] * inverse_freq[None, :]
    cosine_table = jnp.cos(angles)[:, None, :]
    sine_table = jnp.sin(angles)[:, None, :]
    first_half = values[..., :half_rot]
    second_half = values[..., half_rot:ROT]
    return jnp.concatenate(
        [
            first_half * cosine_table - second_half * sine_table,
            second_half * cosine_table + first_half * sine_table,
            values[..., ROT:],
        ],
        -1,
    )


def gelu_piece(values):
    return jax.nn.gelu(values, approximate=True)


def masked_scores(queries, key_rows, family):
    scaling = HEAD_DIM ** (-0.5)
    scores = (
        jnp.einsum("qhd,khd->hqk", queries, key_rows, preferred_element_type=jnp.float32) * scaling
    )
    places = jnp.arange(queries.shape[0])
    allowed = (places[None, :] <= places[:, None]) & (family[:, None] == family[None, :])
    return jnp.where(allowed[None], scores, -1000000000.0)


def forward_row(pieces):
    qkv_rows, family = pieces
    scores = masked_scores(qkv_rows[:, 0], qkv_rows[:, 1], family)
    row_max = jnp.max(scores, -1, keepdims=True)
    weights = jnp.exp(scores - row_max)
    row_total = jnp.sum(weights, -1, keepdims=True)
    prob_low = (weights / row_total).astype(jnp.bfloat16)
    mixed_heads = jnp.einsum(
        "hqk,khd->qhd", prob_low, qkv_rows[:, 2], preferred_element_type=jnp.float32
    )
    return (mixed_heads.astype(jnp.bfloat16), (row_max + jnp.log(row_total))[..., 0])


def backward_row(pieces):
    qkv_rows, family, log_total, d_mixed = pieces
    scaling = HEAD_DIM ** (-0.5)
    queries = qkv_rows[:, 0]
    key_rows = qkv_rows[:, 1]
    value_rows = qkv_rows[:, 2]
    scores = masked_scores(queries, key_rows, family)
    chances = jnp.exp(scores - log_total[..., None])
    d_chances = jnp.einsum("qhd,khd->hqk", d_mixed, value_rows, preferred_element_type=jnp.float32)
    d_scores = (chances * (d_chances - jnp.sum(chances * d_chances, -1, keepdims=True))).astype(
        jnp.bfloat16
    )
    d_value = jnp.einsum(
        "hqk,qhd->khd", chances.astype(jnp.bfloat16), d_mixed, preferred_element_type=jnp.float32
    )
    d_query = (
        jnp.einsum("hqk,khd->qhd", d_scores, key_rows, preferred_element_type=jnp.float32) * scaling
    )
    d_key = (
        jnp.einsum("hqk,qhd->khd", d_scores, queries, preferred_element_type=jnp.float32) * scaling
    )
    return jnp.stack([d_query, d_key, d_value], 1).astype(jnp.bfloat16)


def on_device(
    inputs,
    norm_gain,
    norm_shift,
    qkv_weight,
    out_weight,
    up_weight,
    up_bias,
    down_weight,
    down_bias,
    partners,
    families,
    cotangent,
):
    row_count, place_count, model_width = inputs.shape
    seq_size = lax.axis_size("seq")
    token_count = row_count * place_count
    values = inputs.astype(jnp.float32)
    normed, norm_pull = jax.vjp(norm_piece, values, norm_gain, norm_shift)
    normed_low = normed.astype(jnp.bfloat16).reshape(token_count, model_width)
    raw_qkv = jnp.dot(normed_low, qkv_weight, preferred_element_type=jnp.float32)
    raw_qkv = raw_qkv.reshape(row_count, place_count, 3, HEADS, HEAD_DIM)
    places = lax.axis_index("seq") * place_count + jnp.arange(place_count)

    def rope_piece(raw_values):
        return jnp.stack(
            [
                rotate(raw_values[:, :, 0], places),
                rotate(raw_values[:, :, 1], places),
                raw_values[:, :, 2],
            ],
            2,
        )

    rotated, rope_pull = jax.vjp(rope_piece, raw_qkv)
    outgoing = rotated.astype(jnp.bfloat16).reshape(row_count, place_count, 3, seq_size, -1)
    received = lax.all_to_all(outgoing, "seq", split_axis=3, concat_axis=1, tiled=True)
    full_length = received.shape[1]
    received = received.reshape(row_count, full_length, 3, -1, HEAD_DIM)
    mixed_heads, log_totals = lax.map(forward_row, (received, families))
    group_width = mixed_heads.shape[2] * HEAD_DIM
    returned = lax.all_to_all(
        mixed_heads.reshape(row_count, full_length, 1, group_width),
        "seq",
        split_axis=1,
        concat_axis=2,
        tiled=True,
    )
    heads_low = returned.reshape(token_count, model_width)
    attn_out = jnp.dot(heads_low, out_weight, preferred_element_type=jnp.float32)
    hidden = jnp.dot(normed_low, up_weight, preferred_element_type=jnp.float32) + up_bias
    active, gelu_pull = jax.vjp(gelu_piece, hidden)
    active_low = active.astype(jnp.bfloat16)
    mlp_out = jnp.dot(active_low, down_weight, preferred_element_type=jnp.float32) + down_bias
    layer_out = (
        (values.reshape(token_count, model_width) + attn_out + mlp_out)
        .astype(jnp.bfloat16)
        .reshape(inputs.shape)
    )
    local_rows = partners - lax.axis_index("dp") * row_count
    grad_low = jnp.take(cotangent, local_rows, axis=0).reshape(token_count, model_width)
    down_grad = jnp.einsum("tf,td->fd", active_low, grad_low, preferred_element_type=jnp.float32)
    down_bias_grad = jnp.sum(grad_low.astype(jnp.float32), 0)
    out_grad = jnp.einsum("te,td->ed", heads_low, grad_low, preferred_element_type=jnp.float32)
    d_active = jnp.einsum("td,fd->tf", grad_low, down_weight, preferred_element_type=jnp.float32)
    d_hidden_low = gelu_pull(d_active)[0].astype(jnp.bfloat16)
    up_bias_grad = jnp.sum(d_hidden_low.astype(jnp.float32), 0)
    up_grad = jnp.einsum("td,tf->df", normed_low, d_hidden_low, preferred_element_type=jnp.float32)
    d_heads = jnp.einsum(
        "td,ed->te", grad_low, out_weight, preferred_element_type=jnp.float32
    ).astype(jnp.bfloat16)
    d_heads = d_heads.reshape(row_count, place_count, seq_size, group_width)
    d_heads_split = lax.all_to_all(d_heads, "seq", split_axis=2, concat_axis=1, tiled=True)
    d_heads_split = d_heads_split.reshape(row_count, full_length, -1, HEAD_DIM)
    d_blocks = lax.map(backward_row, (received, families, log_totals, d_heads_split))
    d_blocks = d_blocks.reshape(row_count, full_length, 3, 1, group_width)
    d_rotated = lax.all_to_all(d_blocks, "seq", split_axis=1, concat_axis=3, tiled=True)
    d_rotated = d_rotated.reshape(row_count, place_count, 3, HEADS, HEAD_DIM).astype(jnp.float32)
    d_raw_low = rope_pull(d_rotated)[0].astype(jnp.bfloat16).reshape(token_count, 3 * model_width)
    qkv_grad = jnp.einsum("td,te->de", normed_low, d_raw_low, preferred_element_type=jnp.float32)
    d_normed = jnp.einsum("te,de->td", d_raw_low, qkv_weight, preferred_element_type=jnp.float32)
    d_normed = d_normed + jnp.einsum(
        "tf,df->td", d_hidden_low, up_weight, preferred_element_type=jnp.float32
    )
    d_values, gain_grad, shift_grad = norm_pull(d_normed.reshape(inputs.shape))
    input_grad = grad_low.astype(jnp.float32).reshape(inputs.shape) + d_values
    gain_sum, shift_sum, up_bias_sum, down_bias_sum = lax.psum(
        (gain_grad, shift_grad, up_bias_grad, down_bias_grad), ("dp", "seq")
    )
    partial_sums = (
        lax.psum_scatter(qkv_grad, "seq", scatter_dimension=1, tiled=True),
        lax.psum_scatter(out_grad, "seq", scatter_dimension=1, tiled=True),
        lax.psum_scatter(up_grad, "seq", scatter_dimension=1, tiled=True),
        lax.psum_scatter(down_grad, "seq", scatter_dimension=1, tiled=True),
    )
    qkv_sum, out_sum, up_sum, down_sum = (
        lax.psum_scatter(partial_sums[0], "dp", scatter_dimension=0, tiled=True),
        lax.psum_scatter(partial_sums[1], "dp", scatter_dimension=0, tiled=True),
        lax.psum_scatter(partial_sums[2], "dp", scatter_dimension=0, tiled=True),
        lax.psum_scatter(partial_sums[3], "dp", scatter_dimension=0, tiled=True),
    )
    return (
        layer_out,
        input_grad,
        gain_sum,
        shift_sum,
        qkv_sum,
        out_sum,
        up_sum,
        up_bias_sum,
        down_sum,
        down_bias_sum,
    )


def solution(mesh):
    placed = (
        P("dp", "seq", None),
        P(),
        P(),
        P(),
        P(),
        P(),
        P(),
        P(),
        P(),
        P("dp"),
        P("dp", None),
        P("dp", "seq", None),
    )
    return jax.shard_map(
        on_device,
        mesh=mesh,
        in_specs=placed,
        out_specs=(
            P("dp", "seq", None),
            P("dp", "seq", None),
            P(),
            P(),
            P("dp", "seq"),
            P("dp", "seq"),
            P("dp", "seq"),
            P(),
            P("dp", "seq"),
            P(),
        ),
        check_vma=False,
    )
```

profile of v0, /device:TPU:0, one launch (start us, length us, event | category | flops | bytes accessed | tf_op | source)
XLA Modules:
  0.0 1331.5 jit_solution(15439892296866444212)
XLA Ops:
  18.7 4.5 reshape.390
  26.4 4.7 all-to-all-start.2
  36.0 8.7 copy.107
  48.4 10.8 fusion.39
  78.0 5.8 all-to-all-start
  83.8 4.4 convert_reduce_fusion.1
  92.4 4.4 reshape.391
  96.9 58.3 %all-to-all-done = bf16[4,256,3,4,256]{1,4,0,2,3:T(8,128)(2,1)} async-done(((bf16[4,256,3,4,256]{1,4,0,2,3:T(8,128)(2,1)}), bf16[4,256,3,4,256]{1,4,0,2,3:T(8,128)(2,1)}, u32[]{:S(2)}, u32[]{:S(2)}) %all-to-all-start) | async-done | bytes 6291488 | tf_op jit(solution)/shard_map/all_to_all | solution.py:126
  155.2 10.3 copy.112
  165.4 11.0 reshape.385
  176.4 60.7 %while.22 = (s32[]{:T(128)}, bf16[4,1024,4,64]{1,3,2,0:T(8,128)(2,1)}, f32[4,4,1024]{2,1,0:T(4,128)}, bf16[4,1024,3,4,64]{1,4,3,2,0:T(8,128)(2,1)}, s32[4,1024]{1,0:T(4,128)S(1)}, /*index=5*/s32[]{:T(128)}) while((s32[]{:T(128)}, bf16[4,1024,4,64]{1,3,2,0:T(8,128)(2,1)}, f32[4,4,1024]{2,1,0:T(4,128)}, bf16[4,1024,3,4,64]{1,4,3,2,0:T(8,128)(2,1)}, ...), condition=%wide.region_5.6_spmd, body=%wide.region_2.5_spmd.sunk | while | flops 1127477248 | bytes 59913292 | solution.py:129
  186.0 5.6 fusion.93
  201.2 5.6 fusion.93
  216.3 5.6 fusion.93
  231.5 5.6 fusion.93
  241.4 4.6 all-to-all-start.1
  246.0 208.5 %while.23 = (s32[]{:T(128)}, bf16[4,1024,3,4,64]{1,4,3,2,0:T(8,128)(2,1)}, bf16[4,1024,3,4,64]{1,4,3,2,0:T(8,128)(2,1)}, s32[4,1024]{1,0:T(4,128)S(1)}, f32[4,4,...) while((s32[]{:T(128)}, bf16[4,1024,3,4,64]{1,4,3,2,0:T(8,128)(2,1)}, ...), condition=%wide.region_8.9_spmd, body=%wide.region_6.8_spmd.sunk | while | flops 2731274240 | bytes 196179696 | solution.py:164
  247.6 9.6 fusion.99
  258.5 12.7 multiply_reduce_fusion.5
  271.2 11.9 multiply_convert_fusion.5
  286.6 4.5 fusion.102
  291.2 4.5 fusion.101
  299.7 9.6 fusion.99
  310.6 12.7 multiply_reduce_fusion.5
  323.3 11.9 multiply_convert_fusion.5
  338.7 4.5 fusion.102
  343.2 4.5 fusion.101
  351.8 9.6 fusion.99
  362.7 12.7 multiply_reduce_fusion.5
  375.4 11.9 multiply_convert_fusion.5
  390.8 4.5 fusion.102
  395.4 4.5 fusion.101
  403.9 9.6 fusion.99
  414.8 12.7 multiply_reduce_fusion.5
  427.5 11.9 multiply_convert_fusion.5
  443.0 4.5 fusion.102
  447.5 4.5 fusion.101
  454.5 10.8 copy.118
  465.2 5.2 all-to-all-start.3
  476.3 4.5 fusion.51
  480.8 82.8 %all-to-all-done.3 = bf16[4,1024,3,1,256]{4,0,3,2,1:T(4,128)(2,1)} async-done(((bf16[4,1024,3,1,256]{4,0,3,2,1:T(4,128)(2,1)}), bf16[4,1024,3,1,256]{4,0,3,2,1:T(4,128)(2,1)}, u32[]{:S(2)}, u32[]{:S(2)}) %all-to-all-start.3) | async-done | bytes 6291488 | tf_op jit(solution)/shard_map/all_to_all | solution.py:166
  567.4 6.2 convert_bitcast_fusion
  573.6 12.6 copy.120
  586.2 9.9 fusion.45
  602.5 7.1 add_convert_fusion
  609.6 11.5 copy.121
  621.2 5.0 copy.130
  628.8 9.3 fusion.50
  638.2 18.6 %fusion.48 = f32[1024,4096]{1,0:T(8,128)} fusion(bf16[1024,1024]{1,0:T(8,128)(2,1)} %bitcast.215, bf16[1024,4096]{1,0:T(8,128)(2,1)} %param.21), kind=kOutput, calls=%fused_computation.117 | convolution fusion | flops 8589934592 | bytes 27262976 | tf_op jit(solution)/shard_map/dot_general | solution.py:140
  656.8 26.5 %convert_reduce_fusion = (f32[4096]{0:T(1024)S(1)}, bf16[1024,4096]{1,0:T(8,128)(2,1)}) fusion(f32[1024,4096]{1,0:T(8,128)} %fusion.48, f32[4096]{0:T(1024)S(1)} %copy-done.28, bf16[1024,1024]{1,0:T(8,128)(2,1)} %copy-done.9, bf16[4096,1024]{1,0:T(8,128)(2,1)} %param.23), kind=kOutput, calls=%fused_computation.59 | convolution fusion | flops 8686399488 | bytes 35684352 | tf_op jit(solution)/shard_map/td,fd->tf/dot_general | solution.py:154
  683.3 16.3 %fusion.52 = f32[1024,4096]{1,0:T(8,128)} fusion(bf16[1024,1024]{1,0:T(8,128)(2,1)} %bitcast.216, bf16[1024,4096]{1,0:T(8,128)(2,1)} %get-tuple-element.104), kind=kOutput, calls=%fused_computation.121 | convolution fusion | flops 8589934592 | bytes 27262976 | tf_op jit(solution)/shard_map/td,tf->df/dot_general | solution.py:157
  699.7 20.1 %fusion.43 = f32[4096,1024]{1,0:T(8,128)} fusion(bf16[1024,1024]{1,0:T(8,128)(2,1)} %copy-done.9, f32[1024,4096]{1,0:T(8,128)} %fusion.48, f32[4096]{0:T(1024)S(1)} %copy-done.28), kind=kOutput, calls=%fused_computation.113 | convolution fusion | flops 8631877632 | bytes 35667968 | tf_op jit(solution)/shard_map/tf,td->fd/dot_general | solution.py:151
  720.5 17.9 %reduce-scatter.9.cloned.1.call-done = f32[1024,768]{1,0:T(8,128)} async-done(((f32[1024,3072]{1,0:T(8,128)}), f32[1024,768]{1,0:T(8,128)}) %reduce-scatter.9.cloned.1.call-update) | async-done | bytes 3145744 | tf_op jit(solution)/shard_map/reduce_scatter | solution.py:180
  738.5 128.8 %reduce-scatter.17.cloned.1.call-done = f32[1024,1024]{1,0:T(8,128)} async-done(((f32[1024,4096]{1,0:T(8,128)}), f32[1024,1024]{1,0:T(8,128)}) %reduce-scatter.17.cloned.1.call-update) | async-done | bytes 4194320 | tf_op jit(solution)/shard_map/reduce_scatter | solution.py:182
  867.4 5.9 fusion.47
  873.3 122.5 %reduce-scatter.21.cloned.1.call-done = f32[4096,256]{1,0:T(8,128)} async-done(((f32[4096,1024]{1,0:T(8,128)}), f32[4096,256]{1,0:T(8,128)}) %reduce-scatter.21.cloned.1.call-update) | async-done | bytes 4194320 | tf_op jit(solution)/shard_map/reduce_scatter | solution.py:183
  995.9 19.7 %fusion.38 = bf16[1024,1024]{1,0:T(8,128)(2,1)} fusion(f32[1024,1024]{1,0:T(8,128)} %fusion.47, bf16[4,256,1024]{2,1,0:T(8,128)(2,1)} %param.16, f32[1024]{0:T(1024)S(1)} %copy-done.29, bf16[4096,1024]{1,0:T(8,128)(2,1)} %param.23, f32[1024,4096]{1,0:T(8,128)} %fusion.48, f32[4096]{0:T(1024)S(1)} %copy-done.28), kind=kOutput, calls=%fused_computation.74 | convolution fusion | flops 8637120512 | bytes 33574912 | tf_op jit(solution)/shard_map/dot_general | solution.py:143
  1015.5 10.7 fusion.49
  1026.3 14.2 %fusion.46 = (f32[1024]{0:T(1024)S(1)}, f32[1024,1024]{1,0:T(8,128)S(1)}) fusion(f32[1024,1024]{1,0:T(8,128)S(1)} %fusion.49, bf16[1024,4096]{1,0:T(8,128)(2,1)} %get-tuple-element.104, bf16[1024,4096]{1,0:T(8,128)(2,1)} %param.21), kind=kOutput, calls=%fused_computation.115 | convolution fusion | flops 8592030720 | bytes 25169920 | tf_op jit(solution)/shard_map/tf,df->td/dot_general | solution.py:171
  1043.5 40.4 %all-reduce.9 = (f32[1024]{0:T(1024)}, f32[1024]{0:T(1024)}, f32[4096]{0:T(1024)}, f32[1024]{0:T(1024)}) all-reduce(f32[1024]{0:T(1024)S(1)} %get-tuple-element.73, f32[1024]{0:T(1024)S(1)} %get-tuple-element.130, f32[4096]{0:T(1024)S(1)} %get-tuple-element.103, f32[1024]{0:T(1024)S(1)} %copy-done.26), channel_id=1, replica_groups=mesh['dp'=8,'seq'=4] {'dp','seq'}, use_global_device_ids=true, to_apply=%region_12.13 | all-reduce | flops 7168 | bytes 57344 | tf_op jit(solution)/shard_map/psum | solution.py:176
  1083.9 5.7 convert_add_fusion
  1089.6 51.3 %reduce-scatter.11.cloned.1.call-done = f32[128,768]{1,0:T(8,128)} async-done(((f32[1024,768]{1,0:T(8,128)}), f32[128,768]{1,0:T(8,128)}) %reduce-scatter.11.cloned.1.call-update) | async-done | bytes 393232 | tf_op jit(solution)/shard_map/reduce_scatter | solution.py:186
  1140.9 91.2 %reduce-scatter.19.cloned.1.call-done = f32[128,1024]{1,0:T(8,128)} async-done(((f32[1024,1024]{1,0:T(8,128)}), f32[128,1024]{1,0:T(8,128)}) %reduce-scatter.19.cloned.1.call-update) | async-done | bytes 524304 | tf_op jit(solution)/shard_map/reduce_scatter | solution.py:188
  1232.1 92.3 %reduce-scatter.23.cloned.1.call-done = f32[512,256]{1,0:T(8,128)} async-done(((f32[4096,256]{1,0:T(8,128)}), f32[512,256]{1,0:T(8,128)}) %reduce-scatter.23.cloned.1.call-update) | async-done | bytes 524304 | tf_op jit(solution)/shard_map/reduce_scatter | solution.py:189
  (212 shorter events, 146.3 us)
Async XLA Ops:
  7.2 7.7 copy-start
  13.6 1.3 copy-start.9
  26.4 51.6 %all-to-all-start.2 = ((bf16[4,256,4,256]{3,1,0,2:T(8,128)(2,1)}), bf16[4,256,4,256]{3,1,0,2:T(8,128)(2,1)}, u32[]{:S(2)}, u32[]{:S(2)}) async-start(bf16[4,256,4,256]{3,1,0,2:T(8,128)(2,1)} %copy.116), calls=%async_computation.2 | async-start | bytes 4194304 | tf_op jit(solution)/shard_map/all_to_all | solution.py:162
  33.1 11.6 copy-start.17
  35.4 0.6 copy-start.24
  36.0 8.7 copy-start.20
  36.0 8.7 copy-start.22
  36.0 8.7 copy-start.27
  47.1 1.3 copy-start.10
  69.3 3.2 copy-start.8
  69.5 3.0 copy-start.13
  69.5 3.0 copy-start.15
  72.6 1.6 copy-start.6
  78.0 77.2 %all-to-all-start = ((bf16[4,256,3,4,256]{1,4,0,2,3:T(8,128)(2,1)}), bf16[4,256,3,4,256]{1,4,0,2,3:T(8,128)(2,1)}, u32[]{:S(2)}, u32[]{:S(2)}) async-start(bf16[4,256,3,4,256]{1,4,0,2,3:T(8,128)(2,1)} %copy.127), calls=%async_computation | async-start | bytes 12582912 | tf_op jit(solution)/shard_map/all_to_all | solution.py:126
  165.4 11.0 copy-start.19
  241.4 223.9 %all-to-all-start.1 = ((bf16[4,1024,1,256]{3,0,2,1:T(4,128)(2,1)}), bf16[4,1024,1,256]{3,0,2,1:T(4,128)(2,1)}, u32[]{:S(2)}, u32[]{:S(2)}) async-start(bf16[4,1024,1,256]{3,0,2,1:T(4,128)(2,1)} %copy.113), calls=%async_computation.1 | async-start | bytes 4194304 | tf_op jit(solution)/shard_map/all_to_all | solution.py:131
  247.6 10.9 copy-start.1
  271.2 20.0 %slice-start = ((s8[16777216]{0:T(1024)(128)(4,1)}), s8[4194304]{0:T(1024)(128)(4,1)S(1)}, s32[]{:S(2)}) async-start(s8[16777216]{0:T(1024)(128)(4,1)} %bitcast.198), calls=%async_computation.20 | async-start | bytes 8388608 | tf_op jit(solution)/shard_map/while
  271.2 20.0 %slice-start.1 = ((s8[16777216]{0:T(1024)(128)(4,1)}), s8[4194304]{0:T(1024)(128)(4,1)S(1)}, s32[]{:S(2)}) async-start(s8[16777216]{0:T(1024)(128)(4,1)} %bitcast.198), calls=%async_computation.21 | async-start | bytes 8388608 | tf_op jit(solution)/shard_map/while
  271.2 20.0 %slice-start.2 = ((s8[16777216]{0:T(1024)(128)(4,1)}), s8[4194304]{0:T(1024)(128)(4,1)S(1)}, s32[]{:S(2)}) async-start(s8[16777216]{0:T(1024)(128)(4,1)} %bitcast.198), calls=%async_computation.22 | async-start | bytes 8388608 | tf_op jit(solution)/shard_map/while
  283.1 8.1 slice-start.3
  299.7 10.9 copy-start.1
  323.2 20.0 %slice-start = ((s8[16777216]{0:T(1024)(128)(4,1)}), s8[4194304]{0:T(1024)(128)(4,1)S(1)}, s32[]{:S(2)}) async-start(s8[16777216]{0:T(1024)(128)(4,1)} %bitcast.198), calls=%async_computation.20 | async-start | bytes 8388608 | tf_op jit(solution)/shard_map/while
  323.3 20.0 %slice-start.1 = ((s8[16777216]{0:T(1024)(128)(4,1)}), s8[4194304]{0:T(1024)(128)(4,1)S(1)}, s32[]{:S(2)}) async-start(s8[16777216]{0:T(1024)(128)(4,1)} %bitcast.198), calls=%async_computation.21 | async-start | bytes 8388608 | tf_op jit(solution)/shard_map/while
  323.3 20.0 %slice-start.2 = ((s8[16777216]{0:T(1024)(128)(4,1)}), s8[4194304]{0:T(1024)(128)(4,1)S(1)}, s32[]{:S(2)}) async-start(s8[16777216]{0:T(1024)(128)(4,1)} %bitcast.198), calls=%async_computation.22 | async-start | bytes 8388608 | tf_op jit(solution)/shard_map/while
  335.2 8.1 slice-start.3
  351.8 10.9 copy-start.1
  375.4 20.0 %slice-start = ((s8[16777216]{0:T(1024)(128)(4,1)}), s8[4194304]{0:T(1024)(128)(4,1)S(1)}, s32[]{:S(2)}) async-start(s8[16777216]{0:T(1024)(128)(4,1)} %bitcast.198), calls=%async_computation.20 | async-start | bytes 8388608 | tf_op jit(solution)/shard_map/while
  375.4 20.0 %slice-start.1 = ((s8[16777216]{0:T(1024)(128)(4,1)}), s8[4194304]{0:T(1024)(128)(4,1)S(1)}, s32[]{:S(2)}) async-start(s8[16777216]{0:T(1024)(128)(4,1)} %bitcast.198), calls=%async_computation.21 | async-start | bytes 8388608 | tf_op jit(solution)/shard_map/while
  375.4 20.0 %slice-start.2 = ((s8[16777216]{0:T(1024)(128)(4,1)}), s8[4194304]{0:T(1024)(128)(4,1)S(1)}, s32[]{:S(2)}) async-start(s8[16777216]{0:T(1024)(128)(4,1)} %bitcast.198), calls=%async_computation.22 | async-start | bytes 8388608 | tf_op jit(solution)/shard_map/while
  387.3 8.1 slice-start.3
  403.9 10.9 copy-start.1
  427.5 20.0 %slice-start = ((s8[16777216]{0:T(1024)(128)(4,1)}), s8[4194304]{0:T(1024)(128)(4,1)S(1)}, s32[]{:S(2)}) async-start(s8[16777216]{0:T(1024)(128)(4,1)} %bitcast.198), calls=%async_computation.20 | async-start | bytes 8388608 | tf_op jit(solution)/shard_map/while
  427.5 20.0 %slice-start.1 = ((s8[16777216]{0:T(1024)(128)(4,1)}), s8[4194304]{0:T(1024)(128)(4,1)S(1)}, s32[]{:S(2)}) async-start(s8[16777216]{0:T(1024)(128)(4,1)} %bitcast.198), calls=%async_computation.21 | async-start | bytes 8388608 | tf_op jit(solution)/shard_map/while
  427.5 20.0 %slice-start.2 = ((s8[16777216]{0:T(1024)(128)(4,1)}), s8[4194304]{0:T(1024)(128)(4,1)S(1)}, s32[]{:S(2)}) async-start(s8[16777216]{0:T(1024)(128)(4,1)} %bitcast.198), calls=%async_computation.22 | async-start | bytes 8388608 | tf_op jit(solution)/shard_map/while
  439.4 8.1 slice-start.3
  465.2 98.4 %all-to-all-start.3 = ((bf16[4,1024,3,1,256]{4,0,3,2,1:T(4,128)(2,1)}), bf16[4,1024,3,1,256]{4,0,3,2,1:T(4,128)(2,1)}, u32[]{:S(2)}, u32[]{:S(2)}) async-start(bf16[4,1024,3,1,256]{4,0,3,2,1:T(4,128)(2,1)} %copy.118), calls=%async_computation.3 | async-start | bytes 12582912 | tf_op jit(solution)/shard_map/all_to_all | solution.py:166
  470.5 249.4 %reduce-scatter.13.cloned.1.call-start = ((), (), s32[]{:S(2)}) async-start(), calls=%async_computation.14 | async-start | bytes 5242880 | tf_op jit(solution)/shard_map/reduce_scatter | solution.py:181
  472.8 3.5 copy-start.5
  474.9 1.3 copy-start.12
  480.8 257.6 %reduce-scatter.9.cloned.1.call-start = ((), (), s32[]{:S(2)}) async-start(), calls=%async_computation.12 | async-start | bytes 15728640 | tf_op jit(solution)/shard_map/reduce_scatter | solution.py:180
  596.1 2.8 copy-start.4
  596.1 2.8 copy-start.14
  596.1 2.8 copy-start.16
  621.2 7.6 copy-start.11
  626.2 2.6 copy-start.7
  638.1 18.7 %copy-start.28 = (f32[4096]{0:T(1024)S(1)}, f32[4096]{0:T(1024)}, u32[]{:S(2)}) copy-start(f32[4096]{0:T(1024)} %param.22) | copy-start | bytes 49156
  638.1 229.2 %reduce-scatter.17.cloned.1.call-start = ((), (), s32[]{:S(2)}) async-start(), calls=%async_computation.16 | async-start | bytes 20971520 | tf_op jit(solution)/shard_map/reduce_scatter | solution.py:182
  699.7 296.2 %reduce-scatter.21.cloned.1.call-start = ((), (), s32[]{:S(2)}) async-start(), calls=%async_computation.18 | async-start | bytes 20971520 | tf_op jit(solution)/shard_map/reduce_scatter | solution.py:183
  719.8 369.7 %reduce-scatter.15.cloned.1.call-start = ((), (), s32[]{:S(2)}) async-start(), calls=%async_computation.15 | async-start | bytes 1179648 | tf_op jit(solution)/shard_map/reduce_scatter | solution.py:187
  720.4 420.5 %reduce-scatter.11.cloned.1.call-start = ((), (), s32[]{:S(2)}) async-start(), calls=%async_computation.13 | async-start | bytes 3538944 | tf_op jit(solution)/shard_map/reduce_scatter | solution.py:186
  738.4 493.7 %reduce-scatter.19.cloned.1.call-start = ((), (), s32[]{:S(2)}) async-start(), calls=%async_computation.17 | async-start | bytes 4718592 | tf_op jit(solution)/shard_map/reduce_scatter | solution.py:188
  867.3 457.1 %reduce-scatter.23.cloned.1.call-start = ((), (), s32[]{:S(2)}) async-start(), calls=%async_computation.19 | async-start | bytes 4718592 | tf_op jit(solution)/shard_map/reduce_scatter | solution.py:189
  873.3 122.6 %copy-start.29 = (f32[1024]{0:T(1024)S(1)}, f32[1024]{0:T(1024)}, u32[]{:S(2)}) copy-start(f32[1024]{0:T(1024)} %param.24) | copy-start | bytes 12292
  1026.3 14.2 %copy-start.2 = (bf16[4,256,1024]{2,1,0:T(8,128)(2,1)S(1)}, bf16[4,256,1024]{2,1,0:T(8,128)(2,1)}, u32[]{:S(2)}) copy-start(bf16[4,256,1024]{2,1,0:T(8,128)(2,1)} %param.16) | copy-start | bytes 6291460
  1026.3 14.2 %copy-start.18 = (f32[4,256]{1,0:T(4,128)S(1)}, f32[4,256]{1,0:T(4,128)}, u32[]{:S(2)}) copy-start(f32[4,256]{1,0:T(4,128)} %copy-done.17) | copy-start | bytes 12292
  1026.3 14.2 %copy-start.23 = (f32[1024]{0:T(1024)S(1)}, f32[1024]{0:T(1024)}, u32[]{:S(2)}) copy-start(f32[1024]{0:T(1024)} %param.17) | copy-start | bytes 12292
  1040.5 3.0 copy-start.3
  1040.5 0.9 copy-start.25
  1040.5 0.9 copy-start.21
  1041.5 2.0 copy-start.26
Sparse Core Ops, SparseCore 0:
  480.9 69.5 reduce-scatter.12
  638.2 100.1 reduce-scatter.8
  741.1 126.0 reduce-scatter.16
  869.7 126.0 reduce-scatter.20
  1000.0 63.4 reduce-scatter.14
  1067.6 73.3 reduce-scatter.10
  1145.1 86.9 reduce-scatter.18
  1236.7 87.6 reduce-scatter.22
where the time goes:
time: 1340 us; the launch traced here: 1330 us
  waiting for transfers between devices  646 us (48%)
  matrix products  334 us (25%)
  local copies, waits for them, and re-layouts  152 us (11%)
  other arithmetic  123 us (9%)
  blocking collectives  40.4 us (3%)
  starting transfers between devices  21.1 us (2%)
  between operations  14.8 us (1%)
    reduce_scatter x1, waiting for transfers between devices, on_device(): lax.psum_scatter(up_grad, 'seq', scatter_dimension=1, tiled=True)  129 us
    reduce_scatter x1, waiting for transfers between devices, on_device(): lax.psum_scatter(down_grad, 'seq', scatter_dimension=1, tiled=True)  123 us
    reduce_scatter x1, waiting for transfers between devices, on_device(): lax.psum_scatter(partial_sums[3], 'dp', scatter_dimension=0, tiled=True)  92.3 us
    reduce_scatter x1, waiting for transfers between devices, on_device(): lax.psum_scatter(partial_sums[2], 'dp', scatter_dimension=0, tiled=True)  91.2 us
    all_to_all x1, waiting for transfers between devices, on_device(): lax.all_to_all(d_blocks, 'seq', split_axis=1, concat_axis=3, tiled=True)  82.8 us
    dot_general x8, matrix products, masked_scores(): jnp.einsum('qhd,khd->hqk', queries, key_rows, preferred_element_type=jnp....  62.9 us
    all_to_all x1, waiting for transfers between devices, on_device(): lax.all_to_all(outgoing, 'seq', split_axis=3, concat_axis=1, tiled=True)  58.3 us
    reduce_scatter x1, waiting for transfers between devices, on_device(): lax.psum_scatter(partial_sums[0], 'dp', scatter_dimension=0, tiled=True)  51.3 us
  transfers between devices with their start and end apart: 12, of which 8 were waited for; matrix products, arithmetic and copies ran while one was open for 37% of the time, Pallas kernels for 0%

commit v1 on v0

v1 whole, which is shorter than its diff:
```python
import functools

import jax
import jax.numpy as jnp
from jax import lax
from jax.experimental import pallas as pl
from jax.experimental.pallas import tpu as pltpu
from jax.sharding import PartitionSpec as P

F32 = jnp.float32
BF16 = jnp.bfloat16
HEAD_DIM = 64
ROT = 32
EPS = 1e-05
C0 = 0.7978845608028654
C1 = C0 * 0.044715


def dot(a,b): return lax.dot_general(a,b,(((1,),(0,)),((),())),preferred_element_type=F32)
def dot_nt(a,b): return lax.dot_general(a,b,(((1,),(1,)),((),())),preferred_element_type=F32)
def dot_tn(a,b): return lax.dot_general(a,b,(((0,),(0,)),((),())),preferred_element_type=F32)

def turn(x, c, sa, sb, sign):
    left = pltpu.roll(x, 128 - ROT // 2, 1)
    right = pltpu.roll(x, ROT // 2, 1)
    return x * c + sign * (left * sa + right * sb)

def attn_kernel(x_ref, xt_ref, g_ref, wq_ref, wk_ref, wv_ref, wo_ref, famr_ref, famc_ref, c_ref, sa_ref, sb_ref,
                ao_ref, dn_ref, gq_ref, gk_ref, gv_ref, go_ref,
                q_s, k_s, v_s, do_s, kt_s, vt_s, ht_s, dqt_s, dk_s, dv_s, draw_s, ao_s, dn_s):
    step = pl.program_id(0)
    last = pl.num_programs(0) - 1
    n = x_ref.shape[0]
    tile = 256
    c, sa, sb = c_ref[...], sa_ref[...], sb_ref[...]
    x = x_ref[...]
    q_s[...] = (turn(dot(x, wq_ref[...]), c, sa, sb, 1.0) * HEAD_DIM ** -0.5).astype(BF16)
    k = turn(dot(x, wk_ref[...]), c, sa, sb, 1.0).astype(BF16)
    k_s[...] = k
    kt_s[...] = k.T
    v = dot(x, wv_ref[...]).astype(BF16)
    v_s[...] = v
    vt_s[...] = v.T
    do_s[...] = dot_nt(g_ref[...], wo_ref[...]).astype(BF16)
    lane = lax.broadcasted_iota(jnp.int32, (tile, 128), 1)
    for h in range(2):
        mine = (lane < HEAD_DIM) if h == 0 else (lane >= HEAD_DIM)
        rows = slice(h * HEAD_DIM, (h + 1) * HEAD_DIM)
        for i in reversed(range(n // tile)):
            span = (i + 1) * tile
            here = slice(i * tile, span)
            qh = jnp.where(mine, q_s[here, :], 0).astype(BF16)
            doh = jnp.where(mine, do_s[here, :], 0).astype(BF16)
            st = dot_nt(k_s[0:span, :], qh)
            allowed = famc_ref[0:span, :] == famr_ref[:, here]
            kpos = lax.broadcasted_iota(jnp.int32, (span, tile), 0)
            qpos = lax.broadcasted_iota(jnp.int32, (span, tile), 1) + i * tile
            allowed = allowed & (kpos <= qpos)
            st = jnp.where(allowed, st, -1e9)
            e = jnp.exp(st - jnp.max(st, 0, keepdims=True))
            p = e * (1.0 / jnp.sum(e, 0, keepdims=True))
            pb = p.astype(BF16)
            ht_s[rows, here] = dot(vt_s[rows, 0:span], pb).astype(BF16)
            dpt = dot_nt(v_s[0:span, :], doh)
            ds = (p * (dpt - jnp.sum(p * dpt, 0, keepdims=True))).astype(BF16)
            dqt_s[rows, here] = dot(kt_s[rows, 0:span], ds) * HEAD_DIM ** -0.5
            dv = dot(pb, doh)
            dk = dot(ds, qh)
            if h == 0 and i == n // tile - 1:
                dv_s[...] = dv
                dk_s[...] = dk
            else:
                dv_s[0:span, :] += dv
                dk_s[0:span, :] += dk
    draw_s[:, 0:128] = turn(dqt_s[...].T, c, sa, sb, -1.0).astype(BF16)
    draw_s[:, 128:256] = turn(dk_s[...], c, sa, sb, -1.0).astype(BF16)
    draw_s[:, 256:384] = dv_s[...].astype(BF16)
    grads = dot(xt_ref[...], draw_s[...])
    gq_ref[...] = grads[:, 0:128].astype(gq_ref.dtype)
    gk_ref[...] = grads[:, 128:256].astype(gq_ref.dtype)
    gv_ref[...] = grads[:, 256:384].astype(gq_ref.dtype)
    go_ref[...] = dot(ht_s[...], g_ref[...]).astype(go_ref.dtype)
    w = jnp.concatenate([wq_ref[...], wk_ref[...], wv_ref[...]], 1)
    heads = ht_s[...].T
    for m in range(n // tile):
        here = slice(m * tile, (m + 1) * tile)
        dn = dot_nt(draw_s[here, :], w)
        ao = dot(heads[here, :], wo_ref[...])
        @pl.when(step == 0)
        def _():
            dn_s[here, :] = dn
            ao_s[here, :] = ao
        @pl.when((step > 0) & (step < last))
        def _():
            dn_s[here, :] += dn
            ao_s[here, :] += ao
        @pl.when(step == last)
        def _():
            dn_ref[here, :] = (dn_s[here, :] + dn).astype(dn_ref.dtype)
            ao_ref[here, :] = (ao_s[here, :] + ao).astype(ao_ref.dtype)

def tables(n):
    half = ROT // 2
    inverse_freq = 10000.0 ** (-2.0 * jnp.arange(half).astype(F32) / ROT)
    angles = jnp.arange(n).astype(F32)[:, None] * inverse_freq[None, :]
    cosine, sine = jnp.cos(angles), jnp.sin(angles)
    ones, zeros = jnp.ones((n, HEAD_DIM - ROT), F32), jnp.zeros((n, HEAD_DIM - ROT), F32)
    z = jnp.zeros((n, half), F32)
    c = jnp.concatenate([cosine, cosine, ones], 1)
    sa = jnp.concatenate([-sine, z, zeros], 1)
    sb = jnp.concatenate([z, sine, zeros], 1)
    return tuple(jnp.concatenate([t, t], 1) for t in (c, sa, sb))

def attend(x, xt, g, wqkv, wo, family, tabs):
    n, d = x.shape
    pairs = d // 128
    whole = lambda s: pl.BlockSpec(s, lambda p: (0, 0), pipeline_mode=pl.Buffered(1))
    col = lambda k: pl.BlockSpec((d, 128), lambda p, k=k: (0, p + k * pairs))
    gcol = pl.BlockSpec((d, 128), lambda p: (0, p))
    bf = lambda s: jax.ShapeDtypeStruct(s, BF16)
    return pl.pallas_call(
        attn_kernel,
        out_shape=(bf((n, d)), bf((n, d)), bf((d, d)), bf((d, d)), bf((d, d)), bf((d, d))),
        grid=(pairs,),
        in_specs=[whole((n, d)), whole((d, n)), whole((n, d)), col(0), col(1), col(2), pl.BlockSpec((128, d), lambda p: (p, 0)),
                  whole((1, n)), whole((n, 1)), whole((n, 128)), whole((n, 128)), whole((n, 128))],
        out_specs=(whole((n, d)), whole((n, d)), gcol, gcol, gcol, pl.BlockSpec((128, d), lambda p: (p, 0))),
        scratch_shapes=[pltpu.VMEM((n, 128), BF16)] * 4 + [pltpu.VMEM((128, n), BF16)] * 3
        + [pltpu.VMEM((128, n), F32), pltpu.VMEM((n, 128), F32), pltpu.VMEM((n, 128), F32), pltpu.VMEM((n, 384), BF16),
           pltpu.VMEM((n, d), F32), pltpu.VMEM((n, d), F32)],
        compiler_params=pltpu.CompilerParams(vmem_limit_bytes=56 * 2**20),
        cost_estimate=pl.CostEstimate(flops=70_000_000_000, bytes_accessed=30_000_000, transcendentals=20_000_000),
    )(x, xt, g, wqkv, wqkv, wqkv, wo, family.reshape(1, n), family.reshape(n, 1), *tabs)

def mlp_kernel(x_ref, xt_ref, g_ref, wu_ref, b_ref, wd_ref, y_ref, dn_ref, gu_ref, gd_ref, gb_ref, act_s, dh_s, y_s, dn_s, *, tile):
    step = pl.program_id(0)
    last = pl.num_programs(0) - 1
    n = x_ref.shape[0]
    gb = None
    for m in range(n // tile):
        here = slice(m * tile, (m + 1) * tile)
        v = dot(x_ref[here, :], wu_ref[...]) + b_ref[...]
        vv = v * v
        a = 0.5 + 0.5 * jnp.tanh(v * (C0 + C1 * vv))
        act = v * a
        slope = a + act * (1.0 - a) * (2 * C0 + 6 * C1 * vv)
        act_s[here, :] = act.astype(BF16)
        dh = (dot_nt(g_ref[here, :], wd_ref[...]) * slope).astype(BF16)
        dh_s[here, :] = dh
        part = jnp.sum(dh.astype(F32), 0, keepdims=True)
        gb = part if gb is None else gb + part
    gb_ref[...] = gb
    gu_ref[...] = dot(xt_ref[...], dh_s[...]).astype(gu_ref.dtype)
    gd_ref[...] = dot_tn(act_s[...], g_ref[...]).astype(gd_ref.dtype)
    for m in range(n // tile):
        here = slice(m * tile, (m + 1) * tile)
        y = dot(act_s[here, :], wd_ref[...])
        dn = dot_nt(dh_s[here, :], wu_ref[...])
        @pl.when(step == 0)
        def _():
            y_s[here, :] = y
            dn_s[here, :] = dn
        @pl.when((step > 0) & (step < last))
        def _():
            y_s[here, :] += y
            dn_s[here, :] += dn
        @pl.when(step == last)
        def _():
            y_ref[here, :] = y_s[here, :] + y
            dn_ref[here, :] = dn_s[here, :] + dn
def mlp(x, xt, g, wu, b, wd, F=512, tile=256):
    n, d = x.shape
    f = wu.shape[1]
    whole = lambda s: pl.BlockSpec(s, lambda p: (0, 0), pipeline_mode=pl.Buffered(1))
    sd = jax.ShapeDtypeStruct
    return pl.pallas_call(
        functools.partial(mlp_kernel, tile=tile),
        out_shape=(sd((n, d), F32), sd((n, d), F32), sd((d, f), BF16), sd((f, d), BF16), sd((1, f), F32)),
        grid=(f // F,),
        in_specs=[whole((n, d)), whole((d, n)), whole((n, d)), pl.BlockSpec((d, F), lambda p: (0, p)), pl.BlockSpec((1, F), lambda p: (0, p)),
                  pl.BlockSpec((F, d), lambda p: (p, 0))],
        out_specs=(whole((n, d)), whole((n, d)), pl.BlockSpec((d, F), lambda p: (0, p)), pl.BlockSpec((F, d), lambda p: (p, 0)), pl.BlockSpec((1, F), lambda p: (0, p))),
        scratch_shapes=[pltpu.VMEM((n, F), BF16)] * 2 + [pltpu.VMEM((n, d), F32)] * 2,
        compiler_params=pltpu.CompilerParams(vmem_limit_bytes=56 * 2**20),
        cost_estimate=pl.CostEstimate(flops=52_000_000_000, bytes_accessed=50_000_000, transcendentals=4_000_000),
    )(x, xt, g, wu, b.reshape(1, f), wd)

def normalize(values):
    centered = values - jnp.mean(values, -1, keepdims=True)
    scale = lax.rsqrt(jnp.mean(centered * centered, -1, keepdims=True) + EPS)
    return centered * scale, scale


def on_device(inputs, norm_gain, norm_shift, qkv_weight, out_weight, up_weight, up_bias, down_weight, down_bias,
              partners, families, cotangent):
    row_count, place_count, width = inputs.shape
    tokens = row_count * place_count
    local_rows = partners - lax.axis_index("dp") * row_count
    grad = jnp.take(cotangent, local_rows, axis=0)
    to_rows = functools.partial(lax.all_to_all, axis_name="seq", split_axis=0, concat_axis=1, tiled=True)
    to_places = functools.partial(lax.all_to_all, axis_name="seq", split_axis=1, concat_axis=0, tiled=True)
    row_inputs = to_rows(inputs)
    row_grad = to_rows(grad)
    values = inputs.astype(F32).reshape(tokens, width)
    grad = grad.reshape(tokens, width)
    xhat, scale = normalize(values)
    normed = (xhat * norm_gain + norm_shift).astype(BF16)
    mlp_out, d_normed, up_grad, down_grad, up_bias_grad = mlp(normed, normed.T, grad, up_weight, up_bias, down_weight)
    row_xhat, _ = normalize(row_inputs[0].astype(F32))
    row_normed = (row_xhat * norm_gain + norm_shift).astype(BF16)
    family = lax.dynamic_index_in_dim(families, lax.axis_index("seq"), 0, keepdims=False)
    full = row_normed.shape[0]
    attn_out, d_attn, q_grad, k_grad, v_grad, out_grad = attend(
        row_normed, row_normed.T, row_grad[0], qkv_weight, out_weight, family, tables(full))
    attn_back = to_places(attn_out[None]).reshape(tokens, width).astype(F32)
    d_back = to_places(d_attn[None]).reshape(tokens, width).astype(F32)
    layer_out = (values + attn_back + (mlp_out + down_bias)).astype(BF16).reshape(inputs.shape)
    d_total = d_normed + d_back
    grad32 = grad.astype(F32)
    dx = d_total * norm_gain
    input_grad = grad32 + (dx - jnp.mean(dx, -1, keepdims=True) - xhat * jnp.mean(dx * xhat, -1, keepdims=True)) * scale
    small = (jnp.sum(d_total * xhat, 0), jnp.sum(d_total, 0), up_bias_grad[0], jnp.sum(grad32, 0))
    gain_sum, shift_sum, up_bias_sum, down_bias_sum = lax.psum(small, ("dp", "seq"))

    def scatter(whole):
        part = lax.psum_scatter(whole, "seq", scatter_dimension=1, tiled=True)
        return lax.psum_scatter(part, "dp", scatter_dimension=0, tiled=True).astype(F32)

    down_sum = scatter(down_grad)
    up_sum = scatter(up_grad)
    out_sum = scatter(out_grad)
    qkv_sum = scatter(jnp.concatenate([q_grad, k_grad, v_grad], 1))
    return (layer_out, input_grad.reshape(inputs.shape), gain_sum, shift_sum, qkv_sum, out_sum, up_sum, up_bias_sum,
            down_sum, down_bias_sum)


def solution(mesh):
    rows = P("dp", "seq", None)
    placed = (rows,) + (P(),) * 8 + (P("dp"), P("dp", None), rows)
    grads = P("dp", "seq")
    return jax.shard_map(on_device, mesh=mesh, in_specs=placed,
                         out_specs=(rows, rows, P(), P(), grads, grads, grads, P(), grads, P()), check_vma=False)
```

time: 1340 us -> 764 us (0.57)
  matrix products: 334 us -> 0 us
  waiting for transfers between devices: 646 us -> 343 us
  Pallas kernels: 0 us -> 218 us
  local copies, waits for them, and re-layouts: 152 us -> 46.6 us
  other arithmetic: 123 us -> 76.7 us
    dot_general x40 -> x0, matrix products: 334 us -> none  [the longest x8 62.9 us: masked_scores(): jnp.einsum('qhd,khd->hqk', queries, key_rows, preferred_element_type=jnp....]
    pallas_call x0 -> x2, Pallas kernels: none -> 218 us  [the longest x1 142 us: attend(): pl.pallas_call(attn_kernel, out_shape=(bf((n, d)), bf((n, d)), bf((d, d))...]
    reduce_scatter x8, waiting for transfers between devices: 504 us -> 299 us  [the longest x4 151 us: scatter(): lax.psum_scatter(part, 'dp', scatter_dimension=0, tiled=True).astype(F32)]
    all_to_all x4, waiting for transfers between devices: 141 us -> 42.7 us  [the longest x1 22.4 us: on_device(): attn_back = to_places(attn_out[None]).reshape(tokens, width).astype(F32)]
    convert_element_type x8 -> x6, other arithmetic: 63.3 us -> 11 us  [the longest x4 6.77 us: scatter(): lax.psum_scatter(part, 'dp', scatter_dimension=0, tiled=True).astype(F32)]
    reshape x6 -> x2, local copies, waits for them, and re-layouts: 38.2 us -> 1.04 us  [attend(): family.reshape(n, 1)]
    unnamed x0 -> x6, other arithmetic: none -> 26.9 us
    convert_element_type x2 -> x0, local copies, waits for them, and re-layouts: 24.2 us -> none  [the longest x1 12.6 us: on_device(): d_rotated.reshape(row_count, place_count, 3, HEADS, HEAD_DIM)]
  transfers between devices with their start and end apart: 12 -> 12, of which waited for: 8 -> 9; matrix products, arithmetic and copies ran while one was open for 37% -> 16% of each run, Pallas kernels for 0% -> 10%
where the time goes in v1:
time: 764 us; the launch traced here: 758 us
  waiting for transfers between devices  343 us (45%)
  Pallas kernels  218 us (29%)
  other arithmetic  76.7 us (10%)
  local copies, waits for them, and re-layouts  46.6 us (6%)
  blocking collectives  40.5 us (5%)
  starting transfers between devices  17.9 us (2%)
  between operations  14.8 us (2%)
    reduce_scatter x4, waiting for transfers between devices, scatter(): lax.psum_scatter(part, 'dp', scatter_dimension=0, tiled=True).astype(F32)  151 us
    reduce_scatter x4, waiting for transfers between devices, scatter(): part = lax.psum_scatter(whole, 'seq', scatter_dimension=1, tiled=True)  148 us
    pallas_call x1, Pallas kernels, attend(): pl.pallas_call(attn_kernel, out_shape=(bf((n, d)), bf((n, d)), bf((d, d))...  142 us
    pallas_call x1, Pallas kernels, mlp(): pl.pallas_call(functools.partial(mlp_kernel, tile=tile), out_shape=(sd((n...  76.6 us
    psum x1, blocking collectives, on_device(): lax.psum(small, ('dp', 'seq'))  40.5 us
    unnamed x6, other arithmetic  26.9 us
    all_to_all x1, waiting for transfers between devices, on_device(): attn_back = to_places(attn_out[None]).reshape(tokens, width).astype(F32)  22.4 us
    unnamed x49, local copies, waits for them, and re-layouts  17.7 us
  transfers between devices with their start and end apart: 12, of which 9 were waited for; matrix products, arithmetic and copies ran while one was open for 16% of the time, Pallas kernels for 10%

profile of v1, /device:TPU:0, one launch (start us, length us, event | category | flops | bytes accessed | tf_op | source)
XLA Modules:
  0.0 757.7 jit_solution(5374424799165117826)
XLA Ops:
  7.2 4.6 all-to-all-start
  11.9 2.0 gather_fusion
  13.9 2.1 convert_reduce_fusion
  16.0 2.3 fusion.7
  18.3 3.0 multiply_sine_fusion
  21.3 2.7 convert_reduce_fusion.1
  24.0 14.2 %all-to-all-done = bf16[4,256,1024]{2,1,0:T(8,128)(2,1)} async-done(((bf16[4,256,1024]{2,1,0:T(8,128)(2,1)}), bf16[4,256,1024]{2,1,0:T(8,128)(2,1)}, u32[]{:S(2)}, u32[]{:S(2)}) %all-to-all-start) | async-done | bytes 2097184 | tf_op jit(solution)/shard_map/all_to_all | solution.py:202
  38.2 4.5 all-to-all-start.1
  42.7 0.0 reduce-scatter.13.cloned.1.call-start
  42.8 1.0 copy.36.famc_ref
  43.9 1.8 concatenate.19.sa_ref
  45.7 1.8 concatenate.20.sb_ref
  47.5 1.7 concatenate.18.c_ref
  49.2 0.6 constant_dynamic-slice_fusion.famr_ref
  49.8 1.9 convert_reduce_fusion.2
  51.8 2.3 multiply_reduce_fusion
  54.2 4.3 fusion.5
  58.4 3.9 copy.35.xt_ref
  62.3 6.1 all-to-all-done.1
  68.4 141.5 %shard_map.195 = (bf16[1024,1024]{1,0:T(8,128)(2,1)}, bf16[1024,1024]{1,0:T(8,128)(2,1)}, bf16[1024,1024]{1,0:T(8,128)(2,1)}, bf16[1024,1024]{1,0:T(8,128)(2,1)}...) custom-call(bf16[1024,1024]{1,0:T(8,128)(2,1)} %get-tuple-element.47.x_ref, bf16[1024,1024]{1,0:T(8,128)(2,1)} %copy.35.xt_ref, ...), custom_call_target="tpu_custom_call" | custom-call | flops 70000001024 | bytes 30000000 | tf_op jit(solution)/shard_map/pallas_call | solution.py:121
  209.9 0.0 reduce-scatter.13.cloned.1.call-update
  210.0 0.0 reduce-scatter.9.cloned.1.call-start
  210.0 6.4 pad_maximum_fusion
  216.4 0.0 reduce-scatter.9.cloned.1.call-update
  216.4 0.0 reduce-scatter.17.cloned.1.call-start
  216.5 0.1 broadcast_in_dim.56
  216.6 1.5 copy-done.5
  218.0 1.7 bitcast_select_fusion.g_ref
  219.7 4.0 copy.39.xt_ref
  223.7 76.6 %shard_map.196 = (f32[1024,1024]{1,0:T(8,128)}, f32[1024,1024]{1,0:T(8,128)}, bf16[1024,4096]{1,0:T(8,128)(2,1)}, bf16[4096,1024]{1,0:T(8,128)(2,1)}, f32[1,4096]{1,0:T(1,128)}) custom-call(bf16[1024,1024]{1,0:T(8,128)(2,1)} %get-tuple-element.48.x_ref, bf16[1024,1024]{1,0:T(8,128)(2,1)} %copy.39.xt_ref, bf16[1024,1024]{1,0:T(8,128)(2,1)} %bitcast_select_fusion.g_ref, ...), custom_call_target="tpu_custom_call" | custom-call | flops 51999997952 | bytes 50000000 | tf_op jit(solution)/shard_map/pallas_call | solution.py:176
  300.3 0.0 reduce-scatter.17.cloned.1.call-update
  300.3 0.0 reduce-scatter.21.cloned.1.call-start
  300.4 0.5 reduce-scatter.21.cloned.1.call-update
  300.9 0.0 reduce-scatter.15.cloned.1.call-start
  301.0 0.0 reduce-scatter.13.cloned.1.call-done
  301.0 0.5 reduce-scatter.15.cloned.1.call-update
  301.5 0.0 reduce-scatter.11.cloned.1.call-start
  301.5 2.3 reduce-scatter.9.cloned.1.call-done
  303.8 0.2 reduce-scatter.19.cloned.1.call-start
  304.1 74.1 %reduce-scatter.17.cloned.1.call-done = bf16[1024,1024]{1,0:T(8,128)(2,1)} async-done(((bf16[1024,4096]{1,0:T(8,128)(2,1)}), bf16[1024,1024]{1,0:T(8,128)(2,1)}) %reduce-scatter.17.cloned.1.call-update) | async-done | bytes 2097168 | tf_op jit(solution)/shard_map/reduce_scatter | solution.py:226
  378.2 5.2 copy.51
  383.4 0.5 broadcast.129
  383.9 12.8 %reduce.11 = bf16[1024,1024]{1,0:T(8,128)(2,1)S(1)} reduce(bf16[1024,1,1024]{2,1,0:T(2,128)(2,1)} %bitcast.80, bf16[]{:T(256)} %broadcast.129), dimensions={1}, to_apply=%bitcast.77.reduce_sub_computation | reduce | bytes 4194306
  396.7 2.8 reshape.189
  399.4 3.6 all-to-all-start.3
  403.0 0.0 reduce-scatter.23.cloned.1.call-start
  403.1 71.9 %reduce-scatter.21.cloned.1.call-done = bf16[4096,256]{1,0:T(8,128)(2,1)} async-done(((bf16[4096,1024]{1,0:T(8,128)(2,1)}), bf16[4096,256]{1,0:T(8,128)(2,1)}) %reduce-scatter.21.cloned.1.call-update) | async-done | bytes 2097168 | tf_op jit(solution)/shard_map/reduce_scatter | solution.py:226
  475.0 6.8 copy.52
  481.7 14.1 %reduce.12 = bf16[1024,1024]{1,0:T(8,128)(2,1)} reduce(bf16[1024,1,1024]{2,1,0:T(2,128)(2,1)} %bitcast.81, bf16[]{:T(256)} %broadcast.129), dimensions={1}, to_apply=%bitcast.78.reduce_sub_computation | reduce | bytes 4194306
  495.9 4.5 reshape.187
  500.4 4.8 all-to-all-start.2
  505.1 3.3 reshape.190
  508.5 22.4 %all-to-all-done.2 = bf16[4,2,131072]{2,1,0:T(2,128)(2,1)} async-done(((bf16[4,2,131072]{2,1,0:T(2,128)(2,1)}), bf16[4,2,131072]{2,1,0:T(2,128)(2,1)}, u32[]{:S(2)}, u32[]{:S(2)}) %all-to-all-start.2) | async-done | bytes 2097184 | tf_op jit(solution)/shard_map/all_to_all | solution.py:215
  530.9 5.0 reshape.188
  535.9 7.0 fusion.19
  543.0 40.5 %all-reduce = (f32[1024]{0:T(1024)}, f32[1024]{0:T(1024)}, f32[4096]{0:T(1024)}, f32[1024]{0:T(1024)}) all-reduce(f32[1024]{0:T(1024)S(1)} %get-tuple-element.32, f32[1024]{0:T(1024)S(1)} %get-tuple-element.35, f32[4096]{0:T(1024)S(1)} %bitcast.97, f32[1024]{0:T(1024)S(1)} %copy-done.14), channel_id=1, replica_groups=mesh['dp'=8,'seq'=4] {'dp','seq'}, use_global_device_ids=true, to_apply=%region_7.8 | all-reduce | flops 7168 | bytes 57344 | tf_op jit(solution)/shard_map/psum | solution.py:223
  583.5 9.2 %fusion.18 = (f32[1024,1024]{1,0:T(8,128)}, bf16[1024,1024]{1,0:T(8,128)(2,1)}) fusion(bf16[4,256,1024]{2,1,0:T(8,128)(2,1)} %param.12, f32[1024,1024]{1,0:T(8,128)} %get-tuple-element.42, f32[1024]{0:T(1024)S(1)} %get-tuple-element.56, f32[1024]{0:T(1024)S(1)} %get-tuple-element.57, f32[1024]{0:T(1024)S(1)} %bitcast.91, f32[1024]{0:T(1024)S(1)} %bitcast.94, ...), kind=kLoop, calls=%fused_computation.26 | loop fusion | flops 16777216 | bytes 20997120 | tf_op jit(solution)/shard_map/add | solution.py:221
  592.7 1.5 convert_element_type.110
  594.2 14.4 %reduce-scatter.11.cloned.1.call-done = bf16[128,768]{1,0:T(8,128)(2,1)} async-done(((bf16[1024,768]{1,0:T(8,128)(2,1)}), bf16[128,768]{1,0:T(8,128)(2,1)}) %reduce-scatter.11.cloned.1.call-update) | async-done | bytes 196624 | tf_op jit(solution)/shard_map/reduce_scatter | solution.py:227
  608.6 1.7 convert_element_type.109
  610.3 68.3 %reduce-scatter.19.cloned.1.call-done = bf16[128,1024]{1,0:T(8,128)(2,1)} async-done(((bf16[1024,1024]{1,0:T(8,128)(2,1)}), bf16[128,1024]{1,0:T(8,128)(2,1)}) %reduce-scatter.19.cloned.1.call-update) | async-done | bytes 262160 | tf_op jit(solution)/shard_map/reduce_scatter | solution.py:227
  678.7 1.8 convert_element_type.111
  680.5 68.4 %reduce-scatter.23.cloned.1.call-done = bf16[512,256]{1,0:T(8,128)(2,1)} async-done(((bf16[4096,256]{1,0:T(8,128)(2,1)}), bf16[512,256]{1,0:T(8,128)(2,1)}) %reduce-scatter.23.cloned.1.call-update) | async-done | bytes 262160 | tf_op jit(solution)/shard_map/reduce_scatter | solution.py:227
  748.8 1.8 convert_element_type.112
  (62 shorter events, 0.4 us)
Async XLA Ops:
  7.2 4.7 copy-start
  7.2 4.6 copy-start.19
  7.2 31.0 %all-to-all-start = ((bf16[4,256,1024]{2,1,0:T(8,128)(2,1)}), bf16[4,256,1024]{2,1,0:T(8,128)(2,1)}, u32[]{:S(2)}, u32[]{:S(2)}) async-start(bf16[4,256,1024]{2,1,0:T(8,128)(2,1)} %param.12), calls=%async_computation | async-start | bytes 4194304 | tf_op jit(solution)/shard_map/all_to_all | solution.py:202
  13.9 7.4 copy-start.4
  21.3 21.5 %copy-start.18 = (s32[4,1024]{1,0:T(4,128)S(1)}, s32[4,1024]{1,0:T(4,128)}, u32[]{:S(2)}) copy-start(s32[4,1024]{1,0:T(4,128)} %param.22) | copy-start | bytes 49156
  24.0 19.9 %copy-start.6 = (f32[1024,16]{1,0:T(8,128)S(1)}, f32[1024,16]{1,0:T(8,128)}, u32[]{:S(2)}) copy-start(f32[1024,16]{1,0:T(8,128)} %get-tuple-element.50) | copy-start | bytes 196612
  38.2 30.2 %all-to-all-start.1 = ((bf16[4,256,1024]{2,1,0:T(8,128)(2,1)}), bf16[4,256,1024]{2,1,0:T(8,128)(2,1)}, u32[]{:S(2)}, u32[]{:S(2)}) async-start(bf16[4,256,1024]{2,1,0:T(8,128)(2,1)} %get-tuple-element.41), calls=%async_computation.1 | async-start | bytes 4194304 | tf_op jit(solution)/shard_map/all_to_all | solution.py:203
  42.7 258.3 %reduce-scatter.13.cloned.1.call-start = ((), (), s32[]{:S(2)}) async-start(), calls=%async_computation.14 | async-start | bytes 2621440 | tf_op jit(solution)/shard_map/reduce_scatter | solution.py:226
  42.7 11.4 %copy-start.8 = (f32[1,2,4,128]{3,1,2,0:T(2,128)}, f32[1,2,4,128]{3,1,2,0:T(2,128)S(1)}, u32[]{:S(2)}) copy-start(f32[1,2,4,128]{3,1,2,0:T(2,128)S(1)} %copy.45) | copy-start | bytes 12292
  42.8 11.3 %copy-start.10 = (f32[1,2,4,128]{3,1,2,0:T(2,128)}, f32[1,2,4,128]{3,1,2,0:T(2,128)S(1)}, u32[]{:S(2)}) copy-start(f32[1,2,4,128]{3,1,2,0:T(2,128)S(1)} %copy.44) | copy-start | bytes 12292
  47.4 6.7 copy-start.2
  47.4 6.7 copy-start.12
  47.4 6.7 copy-start.16
  210.0 93.8 %reduce-scatter.9.cloned.1.call-start = ((), (), s32[]{:S(2)}) async-start(), calls=%async_computation.12 | async-start | bytes 7864320 | tf_op jit(solution)/shard_map/reduce_scatter | solution.py:226
  216.4 1.6 copy-start.5
  216.4 161.7 %reduce-scatter.17.cloned.1.call-start = ((), (), s32[]{:S(2)}) async-start(), calls=%async_computation.16 | async-start | bytes 10485760 | tf_op jit(solution)/shard_map/reduce_scatter | solution.py:226
  300.3 174.6 %reduce-scatter.21.cloned.1.call-start = ((), (), s32[]{:S(2)}) async-start(), calls=%async_computation.18 | async-start | bytes 10485760 | tf_op jit(solution)/shard_map/reduce_scatter | solution.py:226
  300.9 77.3 %copy-start.7 = (bf16[1024,1024]{1,0:T(8,128)(2,1)S(1)}, bf16[1024,1024]{1,0:T(8,128)(2,1)}, u32[]{:S(2)}) copy-start(bf16[1024,1024]{1,0:T(8,128)(2,1)} %get-tuple-element.24) | copy-start | bytes 6291460
  300.9 291.8 %reduce-scatter.15.cloned.1.call-start = ((), (), s32[]{:S(2)}) async-start(), calls=%async_computation.15 | async-start | bytes 589824 | tf_op jit(solution)/shard_map/reduce_scatter | solution.py:227
  301.5 307.1 %reduce-scatter.11.cloned.1.call-start = ((), (), s32[]{:S(2)}) async-start(), calls=%async_computation.13 | async-start | bytes 1769472 | tf_op jit(solution)/shard_map/reduce_scatter | solution.py:227
  303.8 374.8 %reduce-scatter.19.cloned.1.call-start = ((), (), s32[]{:S(2)}) async-start(), calls=%async_computation.17 | async-start | bytes 2359296 | tf_op jit(solution)/shard_map/reduce_scatter | solution.py:227
  399.4 101.0 %all-to-all-start.3 = ((bf16[4,2,131072]{2,1,0:T(2,128)(2,1)}), bf16[4,2,131072]{2,1,0:T(2,128)(2,1)S(1)}, u32[]{:S(2)}, u32[]{:S(2)}) async-start(bf16[4,2,131072]{2,1,0:T(2,128)(2,1)} %reshape.189), calls=%async_computation.3 | async-start | bytes 4194304 | tf_op jit(solution)/shard_map/all_to_all | solution.py:216
  403.0 345.8 %reduce-scatter.23.cloned.1.call-start = ((), (), s32[]{:S(2)}) async-start(), calls=%async_computation.19 | async-start | bytes 2359296 | tf_op jit(solution)/shard_map/reduce_scatter | solution.py:227
  500.4 30.5 %all-to-all-start.2 = ((bf16[4,2,131072]{2,1,0:T(2,128)(2,1)}), bf16[4,2,131072]{2,1,0:T(2,128)(2,1)}, u32[]{:S(2)}, u32[]{:S(2)}) async-start(bf16[4,2,131072]{2,1,0:T(2,128)(2,1)} %reshape.187), calls=%async_computation.2 | async-start | bytes 4194304 | tf_op jit(solution)/shard_map/all_to_all | solution.py:215
  508.5 27.4 %copy-start.3 = (bf16[4,256,1024]{2,1,0:T(8,128)(2,1)S(1)}, bf16[4,256,1024]{2,1,0:T(8,128)(2,1)}, u32[]{:S(2)}) copy-start(bf16[4,256,1024]{2,1,0:T(8,128)(2,1)} %param.12) | copy-start | bytes 6291460
  508.5 27.4 %copy-start.9 = (f32[1,2,4,128]{3,1,2,0:T(2,128)S(1)}, f32[1,2,4,128]{3,1,2,0:T(2,128)}, u32[]{:S(2)}) copy-start(f32[1,2,4,128]{3,1,2,0:T(2,128)} %copy-done.8) | copy-start | bytes 12292
  508.5 27.4 %copy-start.11 = (f32[1,2,4,128]{3,1,2,0:T(2,128)S(1)}, f32[1,2,4,128]{3,1,2,0:T(2,128)}, u32[]{:S(2)}) copy-start(f32[1,2,4,128]{3,1,2,0:T(2,128)} %copy-done.10) | copy-start | bytes 12292
  508.5 27.4 %copy-start.13 = (f32[1024]{0:T(1024)S(1)}, f32[1024]{0:T(1024)}, u32[]{:S(2)}) copy-start(f32[1024]{0:T(1024)} %param.13) | copy-start | bytes 12292
  535.9 7.1 copy-start.14
  535.9 7.1 copy-start.15
  535.9 47.5 %copy-start.17 = (f32[1024]{0:T(1024)S(1)}, f32[1024]{0:T(1024)}, u32[]{:S(2)}) copy-start(f32[1024]{0:T(1024)} %param.20) | copy-start | bytes 12292
  583.4 167.2 %copy-start.1 = (bf16[4,256,1024]{2,1,0:T(8,128)(2,1)S(1)}, bf16[4,256,1024]{2,1,0:T(8,128)(2,1)}, u32[]{:S(2)}) copy-start(bf16[4,256,1024]{2,1,0:T(8,128)(2,1)} %param.23) | copy-start | bytes 6291460
Sparse Core Ops, SparseCore 0:
  210.1 32.5 reduce-scatter.12
  245.4 58.3 reduce-scatter.8
  306.4 71.7 reduce-scatter.16
  380.8 94.1 reduce-scatter.20
  478.1 61.9 reduce-scatter.14
  543.8 64.8 reduce-scatter.10
  612.2 66.4 reduce-scatter.18
  682.2 66.5 reduce-scatter.22
